TPU v7x, 32 devices: a whole 2x2x4 slice. The times are simulated.
32 devices in a mesh: pose: 4 (over y, core), slab: 8 (over z, x).
Axes of the slice: x: 2, y: 2, z: 4, core: 2. Of those that a mesh axis runs over, the one named last changes fastest.
Arguments:
- coords: float32 [4, 3, 2048], P('pose'), may hold values from -12 to 12, as said below
- atom_types: int32 [4, 2048], P('pose'), may hold values from 0 to 27
- counts: int32 [4], P('pose'), may hold values from 1024 to 2048, as said below
- labels: int32 [4], P('pose'), may hold values from 0 to 1
- receptor_density: bfloat16 [4, 28, 16, 4096], P('pose', None, 'slab'), may hold values from 0 to 1.5
- type_radii: float32 [28], replicated, may hold values from 1.2 to 2.2
- w_stem: bfloat16 [32, 28, 3, 3, 3], replicated, may hold values from -1.25 to 1.25
- w_one: bfloat16 [32, 32, 3, 3, 3], replicated, may hold values from -0.21875 to 0.21875
- w_two: bfloat16 [32, 32, 3, 3, 3], replicated, may hold values from -0.21875 to 0.21875
- w_head: float32 [32], replicated, may hold values from -8 to 8
Outputs:
- scores: float32 [4], P('pose')
- pose_loss: float32 [4], P('pose')
- atom_grad: float32 [4, 3, 2048], P('pose')
- grad_stem: float32 [32, 28, 3, 3, 3], replicated
- grad_one: float32 [32, 32, 3, 3, 3], replicated
- grad_two: float32 [32, 32, 3, 3, 3], replicated
- grad_head: float32 [32], replicated
Inputs may be any that keep to these rules, and one draw needn't show every extreme that they name: The live atoms of a pose are the first counts[p] slots; every pose has 1024 or more of them, and some pose has all 2048. `coords`: every atom lies inside the box of the grid, 0.75 or more from its faces.
All inputs are finite; a program needn't handle non-finite values.
Results may differ from a plain program's by a relative error of at most 0.005.
The roundings to bfloat16 on the way count: a program that leaves them out, or rounds other values in their place, can miss the bound.
Values may be sent and summed in bfloat16 or wider, within the bound.
No kernel may reach another device: no remote copies, remote signals or barrier semaphores. Data moves between devices by JAX's collectives and lax.ppermute only.
A program may use at most 256 MiB of HBM per device.

v0:
```python
import jax
import jax.numpy as jnp
from jax import lax
from jax.sharding import PartitionSpec as P

NXY = 64
CZ = 2
resolution = 0.375
conv_dims = ("NCDHW", "OIDHW", "NCDHW")
grad_dims = ("CNDHW", "IODHW", "NCDHW")


def extended(cells, sides, width):
    for axis, dim in sides:
        count = lax.axis_size(axis)
        ends = count - 1
        head = lax.slice_in_dim(cells, 0, width, axis=dim)
        tail = lax.slice_in_dim(cells, cells.shape[dim] - width, cells.shape[dim], axis=dim)
        cells = jnp.concatenate(
            [
                lax.ppermute(tail, axis, [(i, (i + 1) % count) for i in range(ends)]),
                cells,
                lax.ppermute(head, axis, [((i + 1) % count, i) for i in range(ends)]),
            ],
            axis=dim,
        )
    return cells


def gauss_table(centres, places, inv_sq):
    offset = centres[None, :, None] - places[:, None, :]
    bumps = jnp.exp(-2.0 * offset * offset * inv_sq[:, None, :])
    return (bumps, 4.0 * offset * inv_sq[:, None, :] * bumps)


def spatial(volume):
    return volume.reshape(volume.shape[0], volume.shape[1], volume.shape[2], NXY, NXY)


def flatten(volume):
    return volume.reshape(volume.shape[0], volume.shape[1], volume.shape[2], NXY * NXY)


def conv_valid(padded, kernel):
    result = lax.conv_general_dilated(
        spatial(padded),
        kernel,
        (1, 1, 1),
        [(0, 0), (1, 1), (1, 1)],
        dimension_numbers=conv_dims,
        preferred_element_type=jnp.float32,
    )
    return flatten(result)


def flipped(kernel):
    return jnp.flip(kernel, (2, 3, 4)).transpose(1, 0, 2, 3, 4)


def kernel_grad(padded, upstream):
    result = lax.conv_general_dilated(
        spatial(padded),
        spatial(upstream),
        (1, 1, 1),
        [(0, 0), (1, 1), (1, 1)],
        dimension_numbers=grad_dims,
        preferred_element_type=jnp.float32,
    )
    return result.transpose(1, 0, 2, 3, 4)


def with_rims(volume):
    return extended(volume, (("slab", 2),), 1)


def to_grid(row_cols, plane_count, type_count):
    pose_count = row_cols.shape[0]
    volume = row_cols.reshape(pose_count, plane_count, NXY, type_count, NXY).transpose(
        0, 3, 1, 2, 4
    )
    return volume.reshape(pose_count, type_count, plane_count, NXY * NXY)


def local(
    coords, atom_types, counts, labels, receptor_density, type_radii, w_stem, w_one, w_two, w_head
):
    pose_count = coords.shape[0]
    atom_count = coords.shape[2]
    type_count = type_radii.shape[0]
    slab_count = lax.axis_size("slab")
    total_depth = CZ * slab_count
    cell_count = total_depth * NXY * NXY
    start_plane = lax.axis_index("slab") * CZ
    highest = lax.Precision.HIGHEST
    centres_xy = (jnp.arange(NXY, dtype=jnp.float32) + 0.5 - 0.5 * NXY) * resolution
    kind_ids = jnp.arange(type_count, dtype=jnp.int32)
    type_hits = (atom_types[:, None, :] == kind_ids[None, :, None]).astype(jnp.float32)
    alive = (jnp.arange(atom_count, dtype=jnp.int32)[None, :] < counts[:, None]).astype(jnp.float32)
    live_types = type_hits * alive[:, None, :]
    radius = jnp.sum(type_hits * type_radii[None, :, None], axis=1)
    inv_sq = 1.0 / (radius * radius)
    gauss_x, slope_x = gauss_table(centres_xy, coords[:, 0], inv_sq)
    gauss_y, slope_y = gauss_table(centres_xy, coords[:, 1], inv_sq)
    across_table = (
        (live_types[:, :, None, :] * gauss_y[:, None])
        .reshape(pose_count, type_count * NXY, atom_count)
        .astype(jnp.bfloat16)
    )
    slope_table = (
        (live_types[:, :, None, :] * slope_y[:, None])
        .reshape(pose_count, type_count * NXY, atom_count)
        .astype(jnp.bfloat16)
    )
    plane_count = CZ + 2 * 0
    planes = start_plane - 0 + jnp.arange(plane_count, dtype=jnp.int32)
    inside = ((planes >= 0) & (planes < total_depth)).astype(jnp.float32)
    centres_z = (planes.astype(jnp.float32) + 0.5 - 0.5 * total_depth) * resolution
    gauss_z, slope_z = gauss_table(centres_z, coords[:, 2], inv_sq)
    gauss_z = gauss_z * inside[None, :, None]
    depth_table = (
        (gauss_z[:, :, None, :] * gauss_x[:, None])
        .reshape(pose_count, plane_count * NXY, atom_count)
        .astype(jnp.bfloat16)
    )
    row_cols = jnp.einsum(
        "pra,pqa->prq", depth_table, across_table, preferred_element_type=jnp.float32
    )
    splat, gauss_z, slope_z, inside = (
        to_grid(row_cols, plane_count, type_count),
        gauss_z,
        slope_z,
        inside,
    )
    density = (splat + receptor_density.astype(jnp.float32)).astype(jnp.bfloat16)
    density_pad = with_rims(density)
    stem_pre = conv_valid(density_pad, w_stem)
    hidden_one = jnp.maximum(stem_pre, 0.0).astype(jnp.bfloat16)
    hidden_pad = with_rims(hidden_one)
    second_pre = conv_valid(hidden_pad, w_one)
    hidden_two = jnp.maximum(second_pre, 0.0).astype(jnp.bfloat16)
    two_pad = with_rims(hidden_two)
    summed = hidden_one.astype(jnp.float32) + conv_valid(two_pad, w_two)
    part_pool = jnp.sum(jnp.maximum(summed, 0.0), axis=(2, 3)) / cell_count
    pooled = lax.psum(part_pool, "slab")
    scores = jnp.sum(pooled * w_head[None, :], axis=1)
    label_sign = (2 * labels - 1).astype(jnp.float32)
    pose_loss = jax.nn.softplus(-label_sign * scores)
    score_grad = -label_sign * jax.nn.sigmoid(-label_sign * scores)
    head_term = jnp.sum(score_grad[:, None] * part_pool, axis=0)
    top_grad = jnp.where(
        summed > 0, (score_grad[:, None] * w_head[None, :])[:, :, None, None], 0.0
    ).astype(jnp.bfloat16)
    grad_two_local = kernel_grad(two_pad, top_grad) / cell_count
    back_two = conv_valid(with_rims(top_grad), flipped(w_two))
    mid_grad = jnp.where(second_pre > 0, back_two, 0.0).astype(jnp.bfloat16)
    grad_one_local = kernel_grad(hidden_pad, mid_grad) / cell_count
    back_one = top_grad.astype(jnp.float32) + conv_valid(with_rims(mid_grad), flipped(w_one))
    stem_grad = jnp.where(stem_pre > 0, back_one, 0.0).astype(jnp.bfloat16)
    grad_stem_local = kernel_grad(density_pad, stem_grad) / cell_count
    density_grad = conv_valid(with_rims(stem_grad), flipped(w_stem)).astype(jnp.bfloat16)
    grid_rows = (
        density_grad.reshape(pose_count, type_count, CZ, NXY, NXY)
        .transpose(0, 2, 3, 1, 4)
        .reshape(pose_count, CZ * NXY, type_count * NXY)
    )
    rows_plain = jnp.einsum(
        "prq,pqa->pra", grid_rows, across_table, preferred_element_type=jnp.float32
    ).reshape(pose_count, CZ, NXY, atom_count)
    rows_slope = jnp.einsum(
        "prq,pqa->pra", grid_rows, slope_table, preferred_element_type=jnp.float32
    ).reshape(pose_count, CZ, NXY, atom_count)
    along_x = jnp.einsum("pzxa,pza,pxa->pa", rows_plain, gauss_z, slope_x, precision=highest)
    along_y = jnp.einsum("pzxa,pza,pxa->pa", rows_slope, gauss_z, gauss_x, precision=highest)
    along_z = jnp.einsum("pzxa,pza,pxa->pa", rows_plain, slope_z, gauss_x, precision=highest)
    local_force = jnp.stack([along_x, along_y, along_z], axis=1)
    atom_grad = lax.psum(local_force, "slab")
    grad_stem, grad_one, grad_two, grad_head = lax.psum(
        (grad_stem_local, grad_one_local, grad_two_local, head_term), ("pose", "slab")
    )
    return (scores, pose_loss, atom_grad, grad_stem, grad_one, grad_two, grad_head)


def solution(mesh):
    return jax.shard_map(
        local,
        mesh=mesh,
        in_specs=(
            P("pose", None, None),
            P("pose", None),
            P("pose"),
            P("pose"),
            P("pose", None, "slab", None),
            P(),
            P(),
            P(),
            P(),
            P(),
        ),
        out_specs=(P("pose"), P("pose"), P("pose", None, None), P(), P(), P(), P()),
        check_vma=False,
    )
```

profile of v0, /device:TPU:0, one launch (start us, length us, event | category | flops | bytes accessed | tf_op | source)
XLA Modules:
  0.0 759.1 jit_solution(6189887699078458096)
XLA Ops:
  22.2 6.3 collective-permute-start
  28.5 10.0 %multiply_convert_fusion = (bf16[28,64,2048]{2,1,0:T(8,128)(2,1)}, bf16[28,64,2048]{2,1,0:T(8,128)(2,1)}) fusion(f32[64,2048]{1,0:T(8,128)S(1)} %get-tuple-element.100, f32[28,2048]{1,0:T(8,128)S(1)} %fusion.158, f32[64,2048]{1,0:T(8,128)S(1)} %get-tuple-element.101), kind=kLoop, calls=%fused_computation | loop fusion | flops 14680064 | bytes 15958016 | tf_op jit(solution)/shard_map/convert_element_type | solution.py:112
  62.9 8.6 %copy.334 = bf16[28,4,64,1,8,9]{0,4,5,2,1,3:T(8,128)(2,1)} copy(bf16[28,4,64,1,8,9]{2,1,5,4,0,3:T(4,128)(2,1)} %bitcast.277) | data formatting | bytes 2064384 | tf_op jit(solution)/shard_map/conv_general_dilated | solution.py:45
  73.1 11.6 %maximum_convert_fusion.1 = (bf16[2,64,8,9,32]{4,2,3,1,0:T(8,128)(2,1)}, f32[2,64,8,9,32]{4,2,3,1,0:T(8,128)}) fusion(pred[8,9]{0,1:T(8,128)(4,1)S(1)} %copy-done.10, bf16[32,28,3,3,3]{1,0,4,3,2:T(8,128)(2,1)S(1)} %copy-done.13, bf16[28,4,64,1,7,2]{0,4,5,2,1,3:T(8,128)(2,1)S(1)} %slice.89, bf16[28,4,64,1,8,9]{0,4,5,2,1,3:T(8,128)(2,1)} %copy.334), kind=kOutput, calls=%fused_computation.94 | convolution fusion | flops 446226432 | bytes 3050824 | tf_op jit(solution)/shard_map/conv_general_dilated | solution.py:45
  97.8 5.8 collective-permute-start.2
  105.7 8.1 %copy.434 = bf16[28,4,64,1,8,8]{0,4,5,2,1,3:T(8,128)(2,1)} copy(bf16[28,4,64,1,8,8]{2,1,5,4,0,3:T(4,128)(2,1)} %get-tuple-element.78) | data formatting | bytes 1835008
  113.9 7.7 %copy.433 = bf16[28,4,64,1,8,8]{0,4,5,2,1,3:T(8,128)(2,1)} copy(bf16[28,4,64,1,8,8]{2,1,5,4,0,3:T(4,128)(2,1)} %get-tuple-element.77) | data formatting | bytes 1835008
  122.7 9.0 %fusion.75 = (bf16[28,4,64,8,9,1]{0,3,5,4,2,1:T(8,128)(2,1)}, bf16[28,4,64,8,9,1]{0,3,5,4,2,1:T(8,128)(2,1)}) fusion(bf16[28,4,64,1,7,1]{0,4,5,2,1,3:T(8,128)(2,1)} %copy.435, bf16[28,4,64,1,8,8]{0,4,5,2,1,3:T(8,128)(2,1)} %copy.434, bf16[28,4,64,1,8,8]{0,4,5,2,1,3:T(8,128)(2,1)} %copy.433, bf16[28,4,64,1,7,1]{0,4,5,2,1,3:T(8,128)(2,1)} %copy.432), kind=kLoop, calls=%fused_computation.77 | loop fusion | flops 6193152 | bytes 4100096 | tf_op jit(solution)/shard_map/reshape | solution.py:37
  131.7 6.8 copy.377
  149.3 6.7 copy.340
  157.5 10.4 %maximum_convert_fusion = (bf16[2,64,8,9,32]{4,2,3,1,0:T(8,128)(2,1)}, f32[2,64,8,9,32]{4,2,3,1,0:T(8,128)}) fusion(pred[8,9]{0,1:T(8,128)(4,1)S(1)} %copy-done.10, bf16[32,32,3,3,3]{1,0,4,3,2:T(8,128)(2,1)S(1)} %copy-done, bf16[32,4,64,1,7,2]{0,4,5,2,1,3:T(8,128)(2,1)S(1)} %slice.93, bf16[32,4,64,1,8,9]{0,4,5,2,1,3:T(8,128)(2,1)} %copy.340), kind=kOutput, calls=%fused_computation.92 | convolution fusion | flops 509804544 | bytes 3233864 | tf_op jit(solution)/shard_map/conv_general_dilated | solution.py:45
  188.3 7.7 %copy.437 = bf16[32,4,64,1,8,8]{0,4,5,2,1,3:T(8,128)(2,1)} copy(bf16[32,4,64,1,8,8]{2,0,5,4,1,3:T(8,128)(2,1)} %get-tuple-element.69) | data formatting | bytes 2097152
  197.0 7.6 %copy.438 = bf16[32,4,64,1,8,8]{0,4,5,2,1,3:T(8,128)(2,1)} copy(bf16[32,4,64,1,8,8]{2,0,5,4,1,3:T(8,128)(2,1)} %get-tuple-element.70) | data formatting | bytes 2097152
  204.7 8.8 %fusion.79 = (bf16[32,4,64,8,9,1]{0,3,5,4,2,1:T(8,128)(2,1)}, bf16[32,4,64,8,9,1]{0,3,5,4,2,1:T(8,128)(2,1)}) fusion(bf16[32,4,64,1,7,1]{0,4,5,2,1,3:T(8,128)(2,1)S(1)} %copy.436, bf16[32,4,64,1,8,8]{0,4,5,2,1,3:T(8,128)(2,1)} %copy.437, bf16[32,4,64,1,7,1]{0,4,5,2,1,3:T(8,128)(2,1)} %copy.439, bf16[32,4,64,1,8,8]{0,4,5,2,1,3:T(8,128)(2,1)} %copy.438), kind=kLoop, calls=%fused_computation.81 | loop fusion | flops 7077888 | bytes 4685824 | tf_op jit(solution)/shard_map/concatenate | solution.py:19
  213.4 5.5 copy.383
  227.5 6.8 copy.346
  235.8 11.3 %select_reduce_fusion = (f32[32]{0:T(128)S(1)}, f32[2,64,8,9,32]{4,2,3,1,0:T(8,128)}) fusion(bf16[2,64,8,9,32]{4,2,3,1,0:T(8,128)(2,1)} %get-tuple-element.109, pred[8,9]{0,1:T(8,128)(4,1)S(1)} %copy-done.10, bf16[32,32,3,3,3]{1,0,4,3,2:T(8,128)(2,1)S(1)} %copy-done.11, bf16[32,4,64,1,7,2]{0,4,5,2,1,3:T(8,128)(2,1)S(1)} %slice.97, ...), kind=kOutput, calls=%fused_computation.91 | convolution fusion | flops 510394336 | bytes 3233992 | tf_op jit(solution)/shard_map/conv_general_dilated | solution.py:45
  247.1 19.5 %psum.42 = f32[1,32]{1,0:T(1,128)S(1)} all-reduce(f32[1,32]{1,0:T(1,128)S(1)} %multiply_bitcast_fusion), channel_id=1, replica_groups=mesh['pose'=4,'slab'=8] {'slab'}, use_global_device_ids=true, to_apply=%region_2.0 | all-reduce | flops 32 | bytes 256 | tf_op jit(solution)/shard_map/psum | solution.py:144
  305.1 7.7 %copy.441 = bf16[32,4,64,1,8,8]{0,4,5,2,1,3:T(8,128)(2,1)} copy(bf16[32,4,64,1,8,8]{2,0,5,4,1,3:T(8,128)(2,1)} %get-tuple-element.65) | data formatting | bytes 2097152
  313.8 7.7 %copy.442 = bf16[32,4,64,1,8,8]{0,4,5,2,1,3:T(8,128)(2,1)} copy(bf16[32,4,64,1,8,8]{2,0,5,4,1,3:T(8,128)(2,1)} %get-tuple-element.66) | data formatting | bytes 2097152
  326.9 36.8 %psum.47 = f32[32]{0:T(128)} all-reduce(f32[32]{0:T(128)S(1)} %broadcast_multiply_fusion.2), channel_id=1, replica_groups=mesh['pose'=4,'slab'=8] {'pose','slab'}, use_global_device_ids=true, to_apply=%region_8.9 | all-reduce | flops 32 | bytes 256 | tf_op jit(solution)/shard_map/psum | solution.py:177
  363.7 9.1 %fusion.81 = (bf16[32,4,64,8,9,1]{0,3,5,4,2,1:T(8,128)(2,1)}, bf16[32,4,64,8,9,1]{0,3,5,4,2,1:T(8,128)(2,1)}) fusion(bf16[32,4,64,1,7,1]{0,4,5,2,1,3:T(8,128)(2,1)S(1)} %copy.440, bf16[32,4,64,1,8,8]{0,4,5,2,1,3:T(8,128)(2,1)} %copy.441, bf16[32,4,64,1,7,1]{0,4,5,2,1,3:T(8,128)(2,1)} %copy.443, bf16[32,4,64,1,8,8]{0,4,5,2,1,3:T(8,128)(2,1)} %copy.442), kind=kLoop, calls=%fused_computation.83 | loop fusion | flops 7077888 | bytes 4685824 | tf_op jit(solution)/shard_map/concatenate | solution.py:19
  372.8 22.9 %fusion.117 = f32[32,32,3,3,3]{0,1,4,3,2:T(8,128)} fusion(bf16[2,64,8,9,32]{4,2,3,1,0:T(8,128)(2,1)S(1)} %copy-done.1, pred[8,9]{0,1:T(8,128)(4,1)S(1)} %copy-done.10, bf16[32,4,64,8,9,1]{0,3,5,4,2,1:T(8,128)(2,1)} %get-tuple-element.121, bf16[32,4,64,8,9,1]{0,3,5,4,2,1:T(8,128)(2,1)} %copy.389, bf16[32,4,64,8,9,1]{0,3,5,4,2,1:T(8,128)(2,1)} %get-tuple-element.120), kind=kOutput, calls=%fused_computation.128 | convolution fusion | flops 515238912 | bytes 4239432 | tf_op jit(solution)/shard_map/transpose | solution.py:69
  408.2 12.1 %select_convert_fusion.1 = bf16[2,64,8,9,32]{4,2,3,1,0:T(8,128)(2,1)} fusion(f32[2,64,8,9,32]{4,2,3,1,0:T(8,128)} %get-tuple-element.112, pred[8,9]{0,1:T(8,128)(4,1)S(1)} %copy-done.10, bf16[32,32,3,3,3]{1,0,4,3,2:T(8,128)(2,1)S(1)} %copy-done.12, bf16[32,4,64,1,7,2]{0,4,5,2,1,3:T(8,128)(2,1)S(1)} %slice.103, bf16[32,4,64,1,8,9]{0,4,5,2,1,3:T(8,128)(2,1)} %copy.355), kind=kOutput, calls=%fused_computation.89 | convolution fusion | flops 510099456 | bytes 3233864 | tf_op jit(solution)/shard_map/conv_general_dilated | solution.py:45
  432.0 23.5 %fusion.127 = f32[32,32,3,3,3]{0,1,4,3,2:T(8,128)} fusion(bf16[2,64,8,9,32]{4,2,3,1,0:T(8,128)(2,1)} %select_convert_fusion.1, pred[8,9]{0,1:T(8,128)(4,1)S(1)} %copy-done.10, bf16[32,4,64,8,9,1]{0,3,5,4,2,1:T(8,128)(2,1)} %get-tuple-element.119, bf16[32,4,64,8,9,1]{0,3,5,4,2,1:T(8,128)(2,1)} %copy.383, bf16[32,4,64,8,9,1]{0,3,5,4,2,1:T(8,128)(2,1)} %get-tuple-element.118), kind=kOutput, calls=%fused_computation.130 | convolution fusion | flops 515238912 | bytes 4239432 | tf_op jit(solution)/shard_map/transpose | solution.py:69
  459.2 5.5 copy.361
  466.2 12.4 %select_convert_fusion = (bf16[2,64,8,9,32]{4,2,3,1,0:T(8,128)(2,1)}, pred[2,64,8,9,32]{4,2,3,1,0:T(8,128)(4,1)S(1)}, f32[2,64,8,9,32]{4,2,3,1,0:T(8,128)}) fusion(bf16[2,64,8,9,32]{4,2,3,1,0:T(8,128)(2,1)} %select_convert_fusion.2, f32[2,64,8,9,32]{4,2,3,1,0:T(8,128)} %get-tuple-element.110, pred[8,9]{0,1:T(8,128)(4,1)S(1)} %copy-done.10, ...), kind=kOutput, calls=%fused_computation.88 | convolution fusion | flops 510689280 | bytes 5298248 | tf_op jit(solution)/shard_map/conv_general_dilated | solution.py:45
  498.5 5.6 collective-permute-start.10
  504.2 23.3 %fusion.137 = f32[32,28,3,3,3]{0,1,4,3,2:T(8,128)} fusion(bf16[2,64,8,9,32]{4,2,3,1,0:T(8,128)(2,1)} %get-tuple-element.63, pred[8,9]{0,1:T(8,128)(4,1)S(1)} %copy-done.10, bf16[28,4,64,8,9,1]{0,3,5,4,2,1:T(8,128)(2,1)} %get-tuple-element.116, bf16[28,4,64,8,9,1]{0,3,5,4,2,1:T(8,128)(2,1)} %copy.377, bf16[28,4,64,8,9,1]{0,3,5,4,2,1:T(8,128)(2,1)} %get-tuple-element.117), kind=kOutput, calls=%fused_computation.132 | convolution fusion | flops 450870912 | bytes 3783240 | tf_op jit(solution)/shard_map/transpose | solution.py:69
  527.6 134.7 %all-reduce.3.cloned.1.call-done = (f32[32,28,3,3,3]{0,1,4,3,2:T(8,128)}, f32[32,32,3,3,3]{0,1,4,3,2:T(8,128)}, f32[32,32,3,3,3]{0,1,4,3,2:T(8,128)}) async-done(((f32[32,28,3,3,3]{0,1,4,3,2:T(8,128)}, f32[32,32,3,3,3]{0,1,4,3,2:T(8,128)}, f32[32,32,3,3,3]{0,1,4,3,2:T(8,128)}), (f32[32,28,3,3,3]{0,1,4,3,2:T(8,128)}, f32[32,32,3,3,3]{0,1,4,3,2:T(8,128)}, ...) | async-done | bytes 317968 | tf_op jit(solution)/shard_map/psum | solution.py:177
  678.9 10.3 %fusion.54 = bf16[2,64,8,9,28]{4,2,3,1,0:T(8,128)(2,1)} fusion(bf16[32,28,3,3,3]{1,0,4,3,2:T(8,128)(2,1)S(1)} %copy-done.14, bf16[32,4,64,1,7,2]{0,4,5,2,1,3:T(8,128)(2,1)S(1)} %slice.112, bf16[32,4,64,1,8,9]{0,4,5,2,1,3:T(8,128)(2,1)} %copy.368), kind=kOutput, calls=%fused_computation.57 | convolution fusion | flops 445587456 | bytes 1973504 | tf_op jit(solution)/shard_map/conv_general_dilated | solution.py:45
  713.1 37.6 %psum.43 = f32[1,3,2048]{2,0,1:T(1,128)} all-reduce(f32[1,3,2048]{2,0,1:T(1,128)S(1)} %pad_maximum_fusion.1), channel_id=1, replica_groups=mesh['pose'=4,'slab'=8] {'slab'}, use_global_device_ids=true, to_apply=%region_4.5 | all-reduce | flops 6144 | bytes 49152 | tf_op jit(solution)/shard_map/psum | solution.py:176
  (183 shorter events, 233.2 us)
Async XLA Ops:
  7.2 150.3 %copy-start = (bf16[32,32,3,3,3]{1,0,4,3,2:T(8,128)(2,1)S(1)}, bf16[32,32,3,3,3]{1,0,4,3,2:T(8,128)(2,1)}, u32[]{:S(2)}) copy-start(bf16[32,32,3,3,3]{1,0,4,3,2:T(8,128)(2,1)} %param.17) | copy-start | bytes 165892
  7.2 655.1 %all-reduce.3.cloned.1.call-start = ((), (), s32[]{:S(2)}) async-start(), calls=%async_computation | async-start | bytes 2654208 | tf_op jit(solution)/shard_map/psum | solution.py:177
  11.9 7.0 copy-start.9
  20.9 21.1 %collective-permute-start.1 = (bf16[1,28,1,4096]{3,2,1,0:T(2,128)(2,1)S(1)}, bf16[1,28,1,4096]{3,2,1,0:T(2,128)(2,1)S(1)}, u32[]{:S(2)}, u32[]{:S(2)}) collective-permute-start(bf16[1,28,1,4096]{3,2,1,0:T(2,128)(2,1)S(1)} %get-tuple-element.94), channel_id=1, source_target_pairs={{1,0},{2,1},{3,2},{4,3},{5,4},{6,5},{7,6},{9,8},{10,9},{11,10},{12... | collective-permute-start | bytes 688136 | tf_op jit(solution)/shard_map/ppermute | solution.py:23
  22.2 24.1 %collective-permute-start = (bf16[1,28,1,4096]{3,2,1,0:T(2,128)(2,1)S(1)}, bf16[1,28,1,4096]{3,2,1,0:T(2,128)(2,1)}, u32[]{:S(2)}, u32[]{:S(2)}) collective-permute-start(bf16[1,28,1,4096]{3,2,1,0:T(2,128)(2,1)S(1)} %get-tuple-element.93), channel_id=1, source_target_pairs={{0,1},{1,2},{2,3},{3,4},{4,5},{5,6},{6,7},{8,9},{9,10},{10,11},{11... | collective-permute-start | bytes 688136 | tf_op jit(solution)/shard_map/ppermute | solution.py:21
  62.9 10.1 %copy-start.10 = (pred[8,9]{0,1:T(8,128)(4,1)S(1)}, pred[8,9]{0,1:T(8,128)(4,1)}, u32[]{:S(2)}) copy-start(pred[8,9]{0,1:T(8,128)(4,1)} %constant.99) | copy-start | bytes 220
  62.9 10.1 %copy-start.13 = (bf16[32,28,3,3,3]{1,0,4,3,2:T(8,128)(2,1)S(1)}, bf16[32,28,3,3,3]{1,0,4,3,2:T(8,128)(2,1)}, u32[]{:S(2)}) copy-start(bf16[32,28,3,3,3]{1,0,4,3,2:T(8,128)(2,1)} %param.16) | copy-start | bytes 145156
  96.5 42.0 %collective-permute-start.3 = (bf16[1,32,1,4096]{3,1,2,0:T(8,128)(2,1)}, bf16[1,32,1,4096]{3,1,2,0:T(8,128)(2,1)}, u32[]{:S(2)}, u32[]{:S(2)}) collective-permute-start(bf16[1,32,1,4096]{3,1,2,0:T(8,128)(2,1)} %get-tuple-element.92), channel_id=1, source_target_pairs={{1,0},{2,1},{3,2},{4,3},{5,4},{6,5},{7,6},{9,8},{10,9},{11,10},{12... | collective-permute-start | bytes 786440 | tf_op jit(solution)/shard_map/ppermute | solution.py:23
  97.8 42.9 %collective-permute-start.2 = (bf16[1,32,1,4096]{3,1,2,0:T(8,128)(2,1)}, bf16[1,32,1,4096]{3,1,2,0:T(8,128)(2,1)}, u32[]{:S(2)}, u32[]{:S(2)}) collective-permute-start(bf16[1,32,1,4096]{3,1,2,0:T(8,128)(2,1)} %get-tuple-element.91), channel_id=1, source_target_pairs={{0,1},{1,2},{2,3},{3,4},{4,5},{5,6},{6,7},{8,9},{9,10},{10,11},{11... | collective-permute-start | bytes 786440 | tf_op jit(solution)/shard_map/ppermute | solution.py:21
  180.3 38.7 %collective-permute-start.5 = (bf16[1,32,1,4096]{3,1,2,0:T(8,128)(2,1)}, bf16[1,32,1,4096]{3,1,2,0:T(8,128)(2,1)}, u32[]{:S(2)}, u32[]{:S(2)}) collective-permute-start(bf16[1,32,1,4096]{3,1,2,0:T(8,128)(2,1)} %get-tuple-element.90), channel_id=1, source_target_pairs={{1,0},{2,1},{3,2},{4,3},{5,4},{6,5},{7,6},{9,8},{10,9},{11,10},{12... | collective-permute-start | bytes 786440 | tf_op jit(solution)/shard_map/ppermute | solution.py:23
  181.6 39.7 %collective-permute-start.4 = (bf16[1,32,1,4096]{3,1,2,0:T(8,128)(2,1)}, bf16[1,32,1,4096]{3,1,2,0:T(8,128)(2,1)}, u32[]{:S(2)}, u32[]{:S(2)}) collective-permute-start(bf16[1,32,1,4096]{3,1,2,0:T(8,128)(2,1)} %get-tuple-element.89), channel_id=1, source_target_pairs={{0,1},{1,2},{2,3},{3,4},{4,5},{5,6},{6,7},{8,9},{9,10},{10,11},{11... | collective-permute-start | bytes 786440 | tf_op jit(solution)/shard_map/ppermute | solution.py:21
  227.5 8.3 %copy-start.11 = (bf16[32,32,3,3,3]{1,0,4,3,2:T(8,128)(2,1)S(1)}, bf16[32,32,3,3,3]{1,0,4,3,2:T(8,128)(2,1)}, u32[]{:S(2)}) copy-start(bf16[32,32,3,3,3]{1,0,4,3,2:T(8,128)(2,1)} %param.18) | copy-start | bytes 165892
  235.8 30.8 %copy-start.15 = (f32[32]{0:T(128)S(1)}, f32[32]{0:T(128)}, u32[]{:S(2)}) copy-start(f32[32]{0:T(128)} %param.19) | copy-start | bytes 388
  276.9 5.4 copy-start.2
  283.9 6.3 copy-start.3
  291.6 0.8 copy-start.4
  293.2 102.6 %collective-permute-start.7 = (bf16[1,32,1,4096]{3,1,2,0:T(8,128)(2,1)}, bf16[1,32,1,4096]{3,1,2,0:T(8,128)(2,1)}, u32[]{:S(2)}, u32[]{:S(2)}) collective-permute-start(bf16[1,32,1,4096]{3,1,2,0:T(8,128)(2,1)} %get-tuple-element.88), channel_id=1, source_target_pairs={{1,0},{2,1},{3,2},{4,3},{5,4},{6,5},{7,6},{9,8},{10,9},{11,10},{12... | collective-permute-start | bytes 786440 | tf_op jit(solution)/shard_map/ppermute | solution.py:23
  298.6 99.5 %collective-permute-start.6 = (bf16[1,32,1,4096]{3,1,2,0:T(8,128)(2,1)}, bf16[1,32,1,4096]{3,1,2,0:T(8,128)(2,1)}, u32[]{:S(2)}, u32[]{:S(2)}) collective-permute-start(bf16[1,32,1,4096]{3,1,2,0:T(8,128)(2,1)} %get-tuple-element.87), channel_id=1, source_target_pairs={{0,1},{1,2},{2,3},{3,4},{4,5},{5,6},{6,7},{8,9},{9,10},{10,11},{11... | collective-permute-start | bytes 786440 | tf_op jit(solution)/shard_map/ppermute | solution.py:21
  363.7 9.1 %copy-start.1 = (bf16[2,64,8,9,32]{4,2,3,1,0:T(8,128)(2,1)S(1)}, bf16[2,64,8,9,32]{4,2,3,1,0:T(8,128)(2,1)}, u32[]{:S(2)}) copy-start(bf16[2,64,8,9,32]{4,2,3,1,0:T(8,128)(2,1)} %select_convert_fusion.2) | copy-start | bytes 1769476
  372.8 23.0 %copy-start.7 = (bf16[2,64,8,9,32]{1,4,3,2,0:T(8,128)(2,1)S(1)}, bf16[2,64,8,9,32]{1,4,3,2,0:T(8,128)(2,1)}, u32[]{:S(2)}) copy-start(bf16[2,64,8,9,32]{1,4,3,2,0:T(8,128)(2,1)} %copy.351) | copy-start | bytes 1769476
  401.3 6.9 copy-start.12
  425.7 29.8 %collective-permute-start.9 = (bf16[1,32,1,4096]{3,1,2,0:T(8,128)(2,1)S(1)}, bf16[1,32,1,4096]{3,1,2,0:T(8,128)(2,1)S(1)}, u32[]{:S(2)}, u32[]{:S(2)}) collective-permute-start(bf16[1,32,1,4096]{3,1,2,0:T(8,128)(2,1)S(1)} %get-tuple-element.86), channel_id=1, source_target_pairs={{1,0},{2,1},{3,2},{4,3},{5,4},{6,5},{7,6},{9,8},{10,9},{11,10},{12... | collective-permute-start | bytes 786440 | tf_op jit(solution)/shard_map/ppermute | solution.py:23
  427.0 29.9 %collective-permute-start.8 = (bf16[1,32,1,4096]{3,1,2,0:T(8,128)(2,1)S(1)}, bf16[1,32,1,4096]{3,1,2,0:T(8,128)(2,1)S(1)}, u32[]{:S(2)}, u32[]{:S(2)}) collective-permute-start(bf16[1,32,1,4096]{3,1,2,0:T(8,128)(2,1)S(1)} %get-tuple-element.85), channel_id=1, source_target_pairs={{0,1},{1,2},{2,3},{3,4},{4,5},{5,6},{6,7},{8,9},{9,10},{10,11},{11... | collective-permute-start | bytes 786440 | tf_op jit(solution)/shard_map/ppermute | solution.py:21
  487.1 5.5 copy-start.5
  494.0 174.2 %collective-permute-start.11 = (bf16[1,32,1,4096]{3,1,2,0:T(8,128)(2,1)S(1)}, bf16[1,32,1,4096]{3,1,2,0:T(8,128)(2,1)S(1)}, u32[]{:S(2)}, u32[]{:S(2)}) collective-permute-start(bf16[1,32,1,4096]{3,1,2,0:T(8,128)(2,1)S(1)} %get-tuple-element.84), channel_id=1, source_target_pairs={{1,0},{2,1},{3,2},{4,3},{5,4},{6,5},{7,6},{9,8},{10,9},{11,10},{12... | collective-permute-start | bytes 786440 | tf_op jit(solution)/shard_map/ppermute | solution.py:23
  498.5 171.1 %collective-permute-start.10 = (bf16[1,32,1,4096]{3,1,2,0:T(8,128)(2,1)S(1)}, bf16[1,32,1,4096]{3,1,2,0:T(8,128)(2,1)S(1)}, u32[]{:S(2)}, u32[]{:S(2)}) collective-permute-start(bf16[1,32,1,4096]{3,1,2,0:T(8,128)(2,1)S(1)} %get-tuple-element.83), channel_id=1, source_target_pairs={{0,1},{1,2},{2,3},{3,4},{4,5},{5,6},{6,7},{8,9},{9,10},{10,11},{11... | collective-permute-start | bytes 786440 | tf_op jit(solution)/shard_map/ppermute | solution.py:21
  671.9 7.0 copy-start.14
  692.8 4.3 copy-start.6
  703.5 7.7 %copy-start.8 = (f32[2048,2]{1,0:T(8,128)S(1)}, f32[2048,2]{1,0:T(8,128)}, u32[]{:S(2)}) copy-start(f32[2048,2]{1,0:T(8,128)} %copy.406) | copy-start | bytes 49156
Sparse Core Ops, SparseCore 0:
  527.6 134.6 all-reduce.2
where the time goes:
time: 770 us; the launch traced here: 759 us
  local copies, waits for them, and re-layouts  254 us (33%)
  matrix products  152 us (20%)
  waiting for transfers between devices  139 us (18%)
  blocking collectives  93.9 us (12%)
  other arithmetic  60.3 us (8%)
  starting transfers between devices  41.2 us (5%)
  between operations  18.6 us (2%)
    psum x1, waiting for transfers between devices, local(): lax.psum((grad_stem_local, grad_one_local, grad_two_local, head_term), ('...  135 us
    transpose x3, matrix products, kernel_grad(): return result.transpose(1, 0, 2, 3, 4)  69.8 us
    conv_general_dilated x19, local copies, waits for them, and re-layouts, conv_valid(): lax.conv_general_dilated(spatial(padded), kernel, (1, 1, 1), [(0, 0), (1,...  69 us
    conv_general_dilated x6, matrix products, conv_valid(): lax.conv_general_dilated(spatial(padded), kernel, (1, 1, 1), [(0, 0), (1,...  68.2 us
    unnamed x49, local copies, waits for them, and re-layouts  64 us
    concatenate x31, local copies, waits for them, and re-layouts, extended(): jnp.concatenate([lax.ppermute(tail, axis, [(i, (i + 1) % count) for i in...  42.7 us
    psum x1, blocking collectives, local(): atom_grad = lax.psum(local_force, 'slab')  37.6 us
    psum x1, blocking collectives, local(): lax.psum((grad_stem_local, grad_one_local, grad_two_local, head_term), ('...  36.8 us
  transfers between devices with their start and end apart: 13, of which 2 were waited for; matrix products, arithmetic and copies ran while one was open for 27% of the time, Pallas kernels for 0%

commit v1 on v0

--- a/solution.py
+++ b/solution.py
@@ -175,7 +175,7 @@
     local_force = jnp.stack([along_x, along_y, along_z], axis=1)
     atom_grad = lax.psum(local_force, "slab")
     grad_stem, grad_one, grad_two, grad_head = lax.psum(
-        (grad_stem_local, grad_one_local, grad_two_local, head_term), ("pose", "slab")
+        lax.psum((grad_stem_local, grad_one_local, grad_two_local, head_term), "slab"), "pose"
     )
     return (scores, pose_loss, atom_grad, grad_stem, grad_one, grad_two, grad_head)
 

time: 770 us -> 640 us (0.83)
  waiting for transfers between devices: 139 us -> 46.4 us
  blocking collectives: 93.9 us -> 61.5 us
    psum x1 -> x2, waiting for transfers between devices: 135 us -> 42 us  [the longest x1 42 us: local(): lax.psum((grad_stem_local, grad_one_local, grad_two_local, head_term), 's...]
    psum x1, blocking collectives: 36.8 us -> 6.2 us  [local(): lax.psum(lax.psum((grad_stem_local, grad_one_local, grad_two_local, head_...]
    unnamed x49 -> x53, local copies, waits for them, and re-layouts: 64 us -> 63.9 us
  transfers between devices with their start and end apart: 13 -> 14, of which waited for: 2 -> 2; matrix products, arithmetic and copies ran while one was open for 27% -> 38% of each run, Pallas kernels for 0% -> 0%
where the time goes in v1:
time: 640 us; the launch traced here: 629 us
  local copies, waits for them, and re-layouts  253 us (40%)
  matrix products  151 us (24%)
  blocking collectives  61.5 us (10%)
  other arithmetic  58.3 us (9%)
  waiting for transfers between devices  46.4 us (7%)
  starting transfers between devices  40.5 us (6%)
  between operations  18.4 us (3%)
    transpose x3, matrix products, kernel_grad(): return result.transpose(1, 0, 2, 3, 4)  69.3 us
    conv_general_dilated x19, local copies, waits for them, and re-layouts, conv_valid(): lax.conv_general_dilated(spatial(padded), kernel, (1, 1, 1), [(0, 0), (1,...  69.2 us
    conv_general_dilated x6, matrix products, conv_valid(): lax.conv_general_dilated(spatial(padded), kernel, (1, 1, 1), [(0, 0), (1,...  68.1 us
    unnamed x53, local copies, waits for them, and re-layouts  63.9 us
    concatenate x31, local copies, waits for them, and re-layouts, extended(): jnp.concatenate([lax.ppermute(tail, axis, [(i, (i + 1) % count) for i in...  42.7 us
    psum x1, waiting for transfers between devices, local(): lax.psum((grad_stem_local, grad_one_local, grad_two_local, head_term), 's...  42 us
    psum x1, blocking collectives, local(): atom_grad = lax.psum(local_force, 'slab')  35.8 us
    ppermute x6, starting transfers between devices, extended(): lax.ppermute(tail, axis, [(i, (i + 1) % count) for i in range(ends)])  32.7 us
  transfers between devices with their start and end apart: 14, of which 2 were waited for; matrix products, arithmetic and copies ran while one was open for 38% of the time, Pallas kernels for 0%

profile of v1, /device:TPU:0, one launch (start us, length us, event | category | flops | bytes accessed | tf_op | source)
XLA Modules:
  0.0 629.2 jit_solution(9186861690643932206)
XLA Ops:
  22.2 6.3 collective-permute-start
  28.5 10.0 %multiply_convert_fusion = (bf16[28,64,2048]{2,1,0:T(8,128)(2,1)}, bf16[28,64,2048]{2,1,0:T(8,128)(2,1)}) fusion(f32[64,2048]{1,0:T(8,128)S(1)} %get-tuple-element.105, f32[28,2048]{1,0:T(8,128)S(1)} %fusion.158, f32[64,2048]{1,0:T(8,128)S(1)} %get-tuple-element.106), kind=kLoop, calls=%fused_computation | loop fusion | flops 14680064 | bytes 15958016 | tf_op jit(solution)/shard_map/convert_element_type | solution.py:112
  63.0 8.6 %copy.334 = bf16[28,4,64,1,8,9]{0,4,5,2,1,3:T(8,128)(2,1)} copy(bf16[28,4,64,1,8,9]{2,1,5,4,0,3:T(4,128)(2,1)} %bitcast.277) | data formatting | bytes 2064384 | tf_op jit(solution)/shard_map/conv_general_dilated | solution.py:45
  73.1 11.7 %maximum_convert_fusion.1 = (bf16[2,64,8,9,32]{4,2,3,1,0:T(8,128)(2,1)}, f32[2,64,8,9,32]{4,2,3,1,0:T(8,128)}) fusion(pred[8,9]{0,1:T(8,128)(4,1)S(1)} %copy-done.11, bf16[32,28,3,3,3]{1,0,4,3,2:T(8,128)(2,1)S(1)} %copy-done.15, bf16[28,4,64,1,7,2]{0,4,5,2,1,3:T(8,128)(2,1)S(1)} %slice.89, bf16[28,4,64,1,8,9]{0,4,5,2,1,3:T(8,128)(2,1)} %copy.334), kind=kOutput, calls=%fused_computation.94 | convolution fusion | flops 446226432 | bytes 3050824 | tf_op jit(solution)/shard_map/conv_general_dilated | solution.py:45
  97.9 5.8 collective-permute-start.2
  105.8 7.9 %copy.434 = bf16[28,4,64,1,8,8]{0,4,5,2,1,3:T(8,128)(2,1)} copy(bf16[28,4,64,1,8,8]{2,1,5,4,0,3:T(4,128)(2,1)} %get-tuple-element.83) | data formatting | bytes 1835008
  113.8 7.7 %copy.433 = bf16[28,4,64,1,8,8]{0,4,5,2,1,3:T(8,128)(2,1)} copy(bf16[28,4,64,1,8,8]{2,1,5,4,0,3:T(4,128)(2,1)} %get-tuple-element.82) | data formatting | bytes 1835008
  122.6 8.9 %fusion.75 = (bf16[28,4,64,8,9,1]{0,3,5,4,2,1:T(8,128)(2,1)}, bf16[28,4,64,8,9,1]{0,3,5,4,2,1:T(8,128)(2,1)}) fusion(bf16[28,4,64,1,7,1]{0,4,5,2,1,3:T(8,128)(2,1)} %copy.435, bf16[28,4,64,1,8,8]{0,4,5,2,1,3:T(8,128)(2,1)} %copy.434, bf16[28,4,64,1,8,8]{0,4,5,2,1,3:T(8,128)(2,1)} %copy.433, bf16[28,4,64,1,7,1]{0,4,5,2,1,3:T(8,128)(2,1)} %copy.432), kind=kLoop, calls=%fused_computation.77 | loop fusion | flops 6193152 | bytes 4100096 | tf_op jit(solution)/shard_map/reshape | solution.py:37
  131.5 6.9 %copy.377 = bf16[28,4,64,8,9,1]{0,3,5,4,2,1:T(8,128)(2,1)} copy(bf16[28,4,64,8,9,1]{2,1,4,3,0,5:T(4,128)(2,1)S(1)} %bitcast.269) | data formatting | bytes 2064384 | tf_op jit(solution)/shard_map/reshape | solution.py:37
  149.3 6.7 %copy.340 = bf16[32,4,64,1,8,9]{0,4,5,2,1,3:T(8,128)(2,1)} copy(bf16[32,4,64,1,8,9]{2,0,5,4,1,3:T(8,128)(2,1)} %bitcast.270) | data formatting | bytes 2359296 | tf_op jit(solution)/shard_map/conv_general_dilated | solution.py:45
  157.5 10.5 %maximum_convert_fusion = (bf16[2,64,8,9,32]{4,2,3,1,0:T(8,128)(2,1)}, f32[2,64,8,9,32]{4,2,3,1,0:T(8,128)}) fusion(pred[8,9]{0,1:T(8,128)(4,1)S(1)} %copy-done.11, bf16[32,32,3,3,3]{1,0,4,3,2:T(8,128)(2,1)S(1)} %copy-done, bf16[32,4,64,1,7,2]{0,4,5,2,1,3:T(8,128)(2,1)S(1)} %slice.93, bf16[32,4,64,1,8,9]{0,4,5,2,1,3:T(8,128)(2,1)} %copy.340), kind=kOutput, calls=%fused_computation.92 | convolution fusion | flops 509804544 | bytes 3233864 | tf_op jit(solution)/shard_map/conv_general_dilated | solution.py:45
  188.5 7.7 %copy.437 = bf16[32,4,64,1,8,8]{0,4,5,2,1,3:T(8,128)(2,1)} copy(bf16[32,4,64,1,8,8]{2,0,5,4,1,3:T(8,128)(2,1)} %get-tuple-element.74) | data formatting | bytes 2097152
  197.3 7.7 %copy.438 = bf16[32,4,64,1,8,8]{0,4,5,2,1,3:T(8,128)(2,1)} copy(bf16[32,4,64,1,8,8]{2,0,5,4,1,3:T(8,128)(2,1)} %get-tuple-element.75) | data formatting | bytes 2097152
  204.9 8.8 %fusion.79 = (bf16[32,4,64,8,9,1]{0,3,5,4,2,1:T(8,128)(2,1)}, bf16[32,4,64,8,9,1]{0,3,5,4,2,1:T(8,128)(2,1)}) fusion(bf16[32,4,64,1,7,1]{0,4,5,2,1,3:T(8,128)(2,1)S(1)} %copy.436, bf16[32,4,64,1,8,8]{0,4,5,2,1,3:T(8,128)(2,1)} %copy.437, bf16[32,4,64,1,7,1]{0,4,5,2,1,3:T(8,128)(2,1)} %copy.439, bf16[32,4,64,1,8,8]{0,4,5,2,1,3:T(8,128)(2,1)} %copy.438), kind=kLoop, calls=%fused_computation.81 | loop fusion | flops 7077888 | bytes 4685824 | tf_op jit(solution)/shard_map/concatenate | solution.py:19
  213.7 5.5 copy.383
  227.8 6.8 %copy.346 = bf16[32,4,64,1,8,9]{0,4,5,2,1,3:T(8,128)(2,1)} copy(bf16[32,4,64,1,8,9]{2,0,5,4,1,3:T(8,128)(2,1)} %bitcast.271) | data formatting | bytes 2359296 | tf_op jit(solution)/shard_map/conv_general_dilated | solution.py:45
  236.1 11.0 %select_reduce_fusion = (f32[32]{0:T(128)S(1)}, f32[2,64,8,9,32]{4,2,3,1,0:T(8,128)}) fusion(bf16[2,64,8,9,32]{4,2,3,1,0:T(8,128)(2,1)} %get-tuple-element.114, pred[8,9]{0,1:T(8,128)(4,1)S(1)} %copy-done.11, bf16[32,32,3,3,3]{1,0,4,3,2:T(8,128)(2,1)S(1)} %copy-done.13, bf16[32,4,64,1,7,2]{0,4,5,2,1,3:T(8,128)(2,1)S(1)} %slice.97, ...), kind=kOutput, calls=%fused_computation.91 | convolution fusion | flops 510394336 | bytes 3233992 | tf_op jit(solution)/shard_map/conv_general_dilated | solution.py:45
  247.2 19.5 %psum.70 = f32[1,32]{1,0:T(1,128)S(1)} all-reduce(f32[1,32]{1,0:T(1,128)S(1)} %multiply_bitcast_fusion), channel_id=1, replica_groups=mesh['pose'=4,'slab'=8] {'slab'}, use_global_device_ids=true, to_apply=%region_2.0 | all-reduce | flops 32 | bytes 256 | tf_op jit(solution)/shard_map/psum | solution.py:144
  305.7 7.7 %copy.441 = bf16[32,4,64,1,8,8]{0,4,5,2,1,3:T(8,128)(2,1)} copy(bf16[32,4,64,1,8,8]{2,0,5,4,1,3:T(8,128)(2,1)} %get-tuple-element.70) | data formatting | bytes 2097152
  314.4 7.7 %copy.442 = bf16[32,4,64,1,8,8]{0,4,5,2,1,3:T(8,128)(2,1)} copy(bf16[32,4,64,1,8,8]{2,0,5,4,1,3:T(8,128)(2,1)} %get-tuple-element.71) | data formatting | bytes 2097152
  327.5 9.3 %fusion.81 = (bf16[32,4,64,8,9,1]{0,3,5,4,2,1:T(8,128)(2,1)}, bf16[32,4,64,8,9,1]{0,3,5,4,2,1:T(8,128)(2,1)}) fusion(bf16[32,4,64,1,7,1]{0,4,5,2,1,3:T(8,128)(2,1)S(1)} %copy.440, bf16[32,4,64,1,8,8]{0,4,5,2,1,3:T(8,128)(2,1)} %copy.441, bf16[32,4,64,1,7,1]{0,4,5,2,1,3:T(8,128)(2,1)} %copy.443, bf16[32,4,64,1,8,8]{0,4,5,2,1,3:T(8,128)(2,1)} %copy.442), kind=kLoop, calls=%fused_computation.83 | loop fusion | flops 7077888 | bytes 4685824 | tf_op jit(solution)/shard_map/concatenate | solution.py:19
  336.8 22.7 %fusion.117 = f32[32,32,3,3,3]{0,1,4,3,2:T(8,128)} fusion(bf16[2,64,8,9,32]{4,2,3,1,0:T(8,128)(2,1)S(1)} %copy-done.1, pred[8,9]{0,1:T(8,128)(4,1)S(1)} %copy-done.11, bf16[32,4,64,8,9,1]{0,3,5,4,2,1:T(8,128)(2,1)} %get-tuple-element.126, bf16[32,4,64,8,9,1]{0,3,5,4,2,1:T(8,128)(2,1)} %copy.389, bf16[32,4,64,8,9,1]{0,3,5,4,2,1:T(8,128)(2,1)} %get-tuple-element.125), kind=kOutput, calls=%fused_computation.128 | convolution fusion | flops 515238912 | bytes 4239432 | tf_op jit(solution)/shard_map/transpose | solution.py:69
  365.1 5.5 copy.355
  372.1 12.1 %select_convert_fusion.1 = bf16[2,64,8,9,32]{4,2,3,1,0:T(8,128)(2,1)} fusion(f32[2,64,8,9,32]{4,2,3,1,0:T(8,128)} %get-tuple-element.117, pred[8,9]{0,1:T(8,128)(4,1)S(1)} %copy-done.11, bf16[32,32,3,3,3]{1,0,4,3,2:T(8,128)(2,1)S(1)} %copy-done.14, bf16[32,4,64,1,7,2]{0,4,5,2,1,3:T(8,128)(2,1)S(1)} %slice.103, bf16[32,4,64,1,8,9]{0,4,5,2,1,3:T(8,128)(2,1)} %copy.355), kind=kOutput, calls=%fused_computation.89 | convolution fusion | flops 510099456 | bytes 3233864 | tf_op jit(solution)/shard_map/conv_general_dilated | solution.py:45
  395.9 23.3 %fusion.127 = f32[32,32,3,3,3]{0,1,4,3,2:T(8,128)} fusion(bf16[2,64,8,9,32]{4,2,3,1,0:T(8,128)(2,1)} %select_convert_fusion.1, pred[8,9]{0,1:T(8,128)(4,1)S(1)} %copy-done.11, bf16[32,4,64,8,9,1]{0,3,5,4,2,1:T(8,128)(2,1)} %get-tuple-element.124, bf16[32,4,64,8,9,1]{0,3,5,4,2,1:T(8,128)(2,1)} %copy.383, bf16[32,4,64,8,9,1]{0,3,5,4,2,1:T(8,128)(2,1)} %get-tuple-element.123), kind=kOutput, calls=%fused_computation.130 | convolution fusion | flops 515238912 | bytes 4239432 | tf_op jit(solution)/shard_map/transpose | solution.py:69
  422.8 5.6 copy.361
  430.0 12.4 %select_convert_fusion = (bf16[2,64,8,9,32]{4,2,3,1,0:T(8,128)(2,1)}, pred[2,64,8,9,32]{4,2,3,1,0:T(8,128)(4,1)S(1)}, f32[2,64,8,9,32]{4,2,3,1,0:T(8,128)}) fusion(bf16[2,64,8,9,32]{4,2,3,1,0:T(8,128)(2,1)} %select_convert_fusion.2, f32[2,64,8,9,32]{4,2,3,1,0:T(8,128)} %get-tuple-element.115, pred[8,9]{0,1:T(8,128)(4,1)S(1)} %copy-done.11, ...), kind=kOutput, calls=%fused_computation.88 | convolution fusion | flops 510689280 | bytes 5298248 | tf_op jit(solution)/shard_map/conv_general_dilated | solution.py:45
  467.3 23.3 %fusion.137 = f32[32,28,3,3,3]{0,1,4,3,2:T(8,128)} fusion(bf16[2,64,8,9,32]{4,2,3,1,0:T(8,128)(2,1)} %get-tuple-element.68, pred[8,9]{0,1:T(8,128)(4,1)S(1)} %copy-done.11, bf16[28,4,64,8,9,1]{0,3,5,4,2,1:T(8,128)(2,1)} %get-tuple-element.121, bf16[28,4,64,8,9,1]{0,3,5,4,2,1:T(8,128)(2,1)} %copy.377, bf16[28,4,64,8,9,1]{0,3,5,4,2,1:T(8,128)(2,1)} %get-tuple-element.122), kind=kOutput, calls=%fused_computation.132 | convolution fusion | flops 450870912 | bytes 3783240 | tf_op jit(solution)/shard_map/transpose | solution.py:69
  501.4 10.4 %fusion.54 = bf16[2,64,8,9,28]{4,2,3,1,0:T(8,128)(2,1)} fusion(bf16[32,28,3,3,3]{1,0,4,3,2:T(8,128)(2,1)S(1)} %copy-done.16, bf16[32,4,64,1,7,2]{0,4,5,2,1,3:T(8,128)(2,1)S(1)} %slice.112, bf16[32,4,64,1,8,9]{0,4,5,2,1,3:T(8,128)(2,1)} %copy.368), kind=kOutput, calls=%fused_computation.57 | convolution fusion | flops 445587456 | bytes 1973504 | tf_op jit(solution)/shard_map/conv_general_dilated | solution.py:45
  531.0 42.0 %all-reduce.6.cloned.1.call-done = (f32[32,28,3,3,3]{0,1,4,3,2:T(8,128)}, f32[32,32,3,3,3]{0,1,4,3,2:T(8,128)}, f32[32,32,3,3,3]{0,1,4,3,2:T(8,128)}) async-done(((f32[32,28,3,3,3]{0,1,4,3,2:T(8,128)}, f32[32,32,3,3,3]{0,1,4,3,2:T(8,128)}, f32[32,32,3,3,3]{0,1,4,3,2:T(8,128)}), (f32[32,28,3,3,3]{0,1,4,3,2:T(8,128)}, f32[32,32,3,3,3]{0,1,4,3,2:T(8,128)}, ...) | async-done | bytes 317968 | tf_op jit(solution)/shard_map/psum | solution.py:178
  573.1 35.8 %all-reduce = (f32[1,3,2048]{2,0,1:T(1,128)}, f32[32]{0:T(128)S(1)}) all-reduce(f32[1,3,2048]{2,0,1:T(1,128)S(1)} %pad_maximum_fusion.1, f32[32]{0:T(128)S(1)} %copy-done.12), channel_id=1, replica_groups=mesh['pose'=4,'slab'=8] {'slab'}, use_global_device_ids=true, to_apply=%region_4.5 | all-reduce | flops 6176 | bytes 49408 | tf_op jit(solution)/shard_map/psum | solution.py:176
  608.8 6.2 psum.79
  (190 shorter events, 228.9 us)
Async XLA Ops:
  7.2 150.3 %copy-start = (bf16[32,32,3,3,3]{1,0,4,3,2:T(8,128)(2,1)S(1)}, bf16[32,32,3,3,3]{1,0,4,3,2:T(8,128)(2,1)}, u32[]{:S(2)}) copy-start(bf16[32,32,3,3,3]{1,0,4,3,2:T(8,128)(2,1)} %param.17) | copy-start | bytes 165892
  7.2 565.8 %all-reduce.6.cloned.1.call-start = ((), (), s32[]{:S(2)}) async-start(), calls=%async_computation | async-start | bytes 2654208 | tf_op jit(solution)/shard_map/psum | solution.py:178
  12.0 7.0 %copy-start.10 = (bf16[1,28,2,4096]{3,2,1,0:T(2,128)(2,1)S(1)}, bf16[1,28,2,4096]{3,2,1,0:T(2,128)(2,1)}, u32[]{:S(2)}) copy-start(bf16[1,28,2,4096]{3,2,1,0:T(2,128)(2,1)} %param.14) | copy-start | bytes 1376260
  20.9 21.1 %collective-permute-start.1 = (bf16[1,28,1,4096]{3,2,1,0:T(2,128)(2,1)S(1)}, bf16[1,28,1,4096]{3,2,1,0:T(2,128)(2,1)S(1)}, u32[]{:S(2)}, u32[]{:S(2)}) collective-permute-start(bf16[1,28,1,4096]{3,2,1,0:T(2,128)(2,1)S(1)} %get-tuple-element.99), channel_id=1, source_target_pairs={{1,0},{2,1},{3,2},{4,3},{5,4},{6,5},{7,6},{9,8},{10,9},{11,10},{12... | collective-permute-start | bytes 688136 | tf_op jit(solution)/shard_map/ppermute | solution.py:23
  22.2 24.1 %collective-permute-start = (bf16[1,28,1,4096]{3,2,1,0:T(2,128)(2,1)S(1)}, bf16[1,28,1,4096]{3,2,1,0:T(2,128)(2,1)}, u32[]{:S(2)}, u32[]{:S(2)}) collective-permute-start(bf16[1,28,1,4096]{3,2,1,0:T(2,128)(2,1)S(1)} %get-tuple-element.98), channel_id=1, source_target_pairs={{0,1},{1,2},{2,3},{3,4},{4,5},{5,6},{6,7},{8,9},{9,10},{10,11},{11... | collective-permute-start | bytes 688136 | tf_op jit(solution)/shard_map/ppermute | solution.py:21
  63.0 10.1 %copy-start.11 = (pred[8,9]{0,1:T(8,128)(4,1)S(1)}, pred[8,9]{0,1:T(8,128)(4,1)}, u32[]{:S(2)}) copy-start(pred[8,9]{0,1:T(8,128)(4,1)} %constant.99) | copy-start | bytes 220
  63.0 10.1 %copy-start.15 = (bf16[32,28,3,3,3]{1,0,4,3,2:T(8,128)(2,1)S(1)}, bf16[32,28,3,3,3]{1,0,4,3,2:T(8,128)(2,1)}, u32[]{:S(2)}) copy-start(bf16[32,28,3,3,3]{1,0,4,3,2:T(8,128)(2,1)} %param.16) | copy-start | bytes 145156
  96.6 41.8 %collective-permute-start.3 = (bf16[1,32,1,4096]{3,1,2,0:T(8,128)(2,1)}, bf16[1,32,1,4096]{3,1,2,0:T(8,128)(2,1)}, u32[]{:S(2)}, u32[]{:S(2)}) collective-permute-start(bf16[1,32,1,4096]{3,1,2,0:T(8,128)(2,1)} %get-tuple-element.97), channel_id=1, source_target_pairs={{1,0},{2,1},{3,2},{4,3},{5,4},{6,5},{7,6},{9,8},{10,9},{11,10},{12... | collective-permute-start | bytes 786440 | tf_op jit(solution)/shard_map/ppermute | solution.py:23
  97.9 42.8 %collective-permute-start.2 = (bf16[1,32,1,4096]{3,1,2,0:T(8,128)(2,1)}, bf16[1,32,1,4096]{3,1,2,0:T(8,128)(2,1)}, u32[]{:S(2)}, u32[]{:S(2)}) collective-permute-start(bf16[1,32,1,4096]{3,1,2,0:T(8,128)(2,1)} %get-tuple-element.96), channel_id=1, source_target_pairs={{0,1},{1,2},{2,3},{3,4},{4,5},{5,6},{6,7},{8,9},{9,10},{10,11},{11... | collective-permute-start | bytes 786440 | tf_op jit(solution)/shard_map/ppermute | solution.py:21
  180.5 38.8 %collective-permute-start.5 = (bf16[1,32,1,4096]{3,1,2,0:T(8,128)(2,1)}, bf16[1,32,1,4096]{3,1,2,0:T(8,128)(2,1)}, u32[]{:S(2)}, u32[]{:S(2)}) collective-permute-start(bf16[1,32,1,4096]{3,1,2,0:T(8,128)(2,1)} %get-tuple-element.95), channel_id=1, source_target_pairs={{1,0},{2,1},{3,2},{4,3},{5,4},{6,5},{7,6},{9,8},{10,9},{11,10},{12... | collective-permute-start | bytes 786440 | tf_op jit(solution)/shard_map/ppermute | solution.py:23
  181.8 39.8 %collective-permute-start.4 = (bf16[1,32,1,4096]{3,1,2,0:T(8,128)(2,1)}, bf16[1,32,1,4096]{3,1,2,0:T(8,128)(2,1)}, u32[]{:S(2)}, u32[]{:S(2)}) collective-permute-start(bf16[1,32,1,4096]{3,1,2,0:T(8,128)(2,1)} %get-tuple-element.94), channel_id=1, source_target_pairs={{0,1},{1,2},{2,3},{3,4},{4,5},{5,6},{6,7},{8,9},{9,10},{10,11},{11... | collective-permute-start | bytes 786440 | tf_op jit(solution)/shard_map/ppermute | solution.py:21
  227.8 8.3 %copy-start.13 = (bf16[32,32,3,3,3]{1,0,4,3,2:T(8,128)(2,1)S(1)}, bf16[32,32,3,3,3]{1,0,4,3,2:T(8,128)(2,1)}, u32[]{:S(2)}) copy-start(bf16[32,32,3,3,3]{1,0,4,3,2:T(8,128)(2,1)} %param.18) | copy-start | bytes 165892
  236.1 30.6 %copy-start.17 = (f32[32]{0:T(128)S(1)}, f32[32]{0:T(128)}, u32[]{:S(2)}) copy-start(f32[32]{0:T(128)} %param.19) | copy-start | bytes 388
  277.0 5.4 copy-start.2
  284.0 6.3 %copy-start.3 = (bf16[1,32,2,4096]{3,1,2,0:T(8,128)(2,1)S(1)}, bf16[1,32,2,4096]{3,1,2,0:T(8,128)(2,1)}, u32[]{:S(2)}) copy-start(bf16[1,32,2,4096]{3,1,2,0:T(8,128)(2,1)} %convert_element_type.225) | copy-start | bytes 1572868
  291.7 0.8 copy-start.4
  293.3 66.3 %collective-permute-start.7 = (bf16[1,32,1,4096]{3,1,2,0:T(8,128)(2,1)}, bf16[1,32,1,4096]{3,1,2,0:T(8,128)(2,1)}, u32[]{:S(2)}, u32[]{:S(2)}) collective-permute-start(bf16[1,32,1,4096]{3,1,2,0:T(8,128)(2,1)} %get-tuple-element.93), channel_id=1, source_target_pairs={{1,0},{2,1},{3,2},{4,3},{5,4},{6,5},{7,6},{9,8},{10,9},{11,10},{12... | collective-permute-start | bytes 786440 | tf_op jit(solution)/shard_map/ppermute | solution.py:23
  298.7 63.2 %collective-permute-start.6 = (bf16[1,32,1,4096]{3,1,2,0:T(8,128)(2,1)}, bf16[1,32,1,4096]{3,1,2,0:T(8,128)(2,1)}, u32[]{:S(2)}, u32[]{:S(2)}) collective-permute-start(bf16[1,32,1,4096]{3,1,2,0:T(8,128)(2,1)} %get-tuple-element.92), channel_id=1, source_target_pairs={{0,1},{1,2},{2,3},{3,4},{4,5},{5,6},{6,7},{8,9},{9,10},{10,11},{11... | collective-permute-start | bytes 786440 | tf_op jit(solution)/shard_map/ppermute | solution.py:21
  327.5 9.3 %copy-start.1 = (bf16[2,64,8,9,32]{4,2,3,1,0:T(8,128)(2,1)S(1)}, bf16[2,64,8,9,32]{4,2,3,1,0:T(8,128)(2,1)}, u32[]{:S(2)}) copy-start(bf16[2,64,8,9,32]{4,2,3,1,0:T(8,128)(2,1)} %select_convert_fusion.2) | copy-start | bytes 1769476
  336.8 22.7 %copy-start.7 = (bf16[2,64,8,9,32]{1,4,3,2,0:T(8,128)(2,1)S(1)}, bf16[2,64,8,9,32]{1,4,3,2,0:T(8,128)(2,1)}, u32[]{:S(2)}) copy-start(bf16[2,64,8,9,32]{1,4,3,2,0:T(8,128)(2,1)} %copy.351) | copy-start | bytes 1769476
  365.1 7.0 %copy-start.14 = (bf16[32,32,3,3,3]{1,0,4,3,2:T(8,128)(2,1)S(1)}, bf16[32,32,3,3,3]{1,0,4,3,2:T(8,128)(2,1)}, u32[]{:S(2)}) copy-start(bf16[32,32,3,3,3]{1,0,4,3,2:T(8,128)(2,1)} %param.18) | copy-start | bytes 165892
  389.6 29.6 %collective-permute-start.9 = (bf16[1,32,1,4096]{3,1,2,0:T(8,128)(2,1)S(1)}, bf16[1,32,1,4096]{3,1,2,0:T(8,128)(2,1)S(1)}, u32[]{:S(2)}, u32[]{:S(2)}) collective-permute-start(bf16[1,32,1,4096]{3,1,2,0:T(8,128)(2,1)S(1)} %get-tuple-element.91), channel_id=1, source_target_pairs={{1,0},{2,1},{3,2},{4,3},{5,4},{6,5},{7,6},{9,8},{10,9},{11,10},{12... | collective-permute-start | bytes 786440 | tf_op jit(solution)/shard_map/ppermute | solution.py:23
  390.9 29.6 %collective-permute-start.8 = (bf16[1,32,1,4096]{3,1,2,0:T(8,128)(2,1)S(1)}, bf16[1,32,1,4096]{3,1,2,0:T(8,128)(2,1)S(1)}, u32[]{:S(2)}, u32[]{:S(2)}) collective-permute-start(bf16[1,32,1,4096]{3,1,2,0:T(8,128)(2,1)S(1)} %get-tuple-element.90), channel_id=1, source_target_pairs={{0,1},{1,2},{2,3},{3,4},{4,5},{5,6},{6,7},{8,9},{9,10},{10,11},{11... | collective-permute-start | bytes 786440 | tf_op jit(solution)/shard_map/ppermute | solution.py:21
  450.8 5.5 copy-start.5
  457.8 32.9 %collective-permute-start.11 = (bf16[1,32,1,4096]{3,1,2,0:T(8,128)(2,1)S(1)}, bf16[1,32,1,4096]{3,1,2,0:T(8,128)(2,1)S(1)}, u32[]{:S(2)}, u32[]{:S(2)}) collective-permute-start(bf16[1,32,1,4096]{3,1,2,0:T(8,128)(2,1)S(1)} %get-tuple-element.89), channel_id=1, source_target_pairs={{1,0},{2,1},{3,2},{4,3},{5,4},{6,5},{7,6},{9,8},{10,9},{11,10},{12... | collective-permute-start | bytes 786440 | tf_op jit(solution)/shard_map/ppermute | solution.py:23
  462.3 29.8 %collective-permute-start.10 = (bf16[1,32,1,4096]{3,1,2,0:T(8,128)(2,1)S(1)}, bf16[1,32,1,4096]{3,1,2,0:T(8,128)(2,1)S(1)}, u32[]{:S(2)}, u32[]{:S(2)}) collective-permute-start(bf16[1,32,1,4096]{3,1,2,0:T(8,128)(2,1)S(1)} %get-tuple-element.88), channel_id=1, source_target_pairs={{0,1},{1,2},{2,3},{3,4},{4,5},{5,6},{6,7},{8,9},{9,10},{10,11},{11... | collective-permute-start | bytes 786440 | tf_op jit(solution)/shard_map/ppermute | solution.py:21
  490.6 124.4 %all-reduce.8.cloned.1.call-start = ((), (), s32[]{:S(2)}) async-start(), calls=%async_computation.1 | async-start | bytes 2654208 | tf_op jit(solution)/shard_map/psum | solution.py:177
  494.4 7.0 %copy-start.16 = (bf16[32,28,3,3,3]{1,0,4,3,2:T(8,128)(2,1)S(1)}, bf16[32,28,3,3,3]{1,0,4,3,2:T(8,128)(2,1)}, u32[]{:S(2)}) copy-start(bf16[32,28,3,3,3]{1,0,4,3,2:T(8,128)(2,1)} %param.16) | copy-start | bytes 145156
  515.3 4.3 copy-start.6
  524.6 4.5 copy-start.9
  529.1 1.2 copy-start.8
  529.1 43.9 %copy-start.12 = (f32[32]{0:T(128)S(1)}, f32[32]{0:T(128)}, u32[]{:S(2)}) copy-start(f32[32]{0:T(128)} %broadcast_multiply_fusion.2) | copy-start | bytes 388
Sparse Core Ops, SparseCore 0:
  490.7 82.2 all-reduce.5
  575.6 38.7 all-reduce.7
